TPU v7x, 128 devices: a whole 4x4x4 slice. The times are simulated.
128 devices in a mesh: fsdp: 16 (over x, y_lo, core), tensor: 8 (over y_hi, z).
Axes of the slice: x: 4, y: 4 (y_hi: 2, y_lo: 2; y = y_hi * 2 + y_lo), z: 4, core: 2. Of those that a mesh axis runs over, the one named last changes fastest.
Arguments:
- tokens: bfloat16 [2048, 8192], P('tensor', 'fsdp'), may hold values from -6 to 6
- gate_weight: bfloat16 [8192, 14336], P('fsdp', 'tensor'), may hold values from -0.0625 to 0.0625
- up_weight: bfloat16 [8192, 14336], P('fsdp', 'tensor'), may hold values from -0.0625 to 0.0625
- down_frozen: bfloat16 [14336, 8192], P('tensor', 'fsdp'), may hold values from -0.046875 to 0.046875
- down_learn: bfloat16 [14336, 8192], P('tensor', 'fsdp'), may hold values from -0.046875 to 0.046875
- steer: float32 [8192], replicated, may hold values from -6 to 6
- sample_lengths: int32 [2, 8], replicated, may hold values from 1 to 128, 640 in all within a row
Outputs:
- grad_down: float32 [14336, 8192], P('tensor', 'fsdp')
- losses: float32 [2], replicated
Inputs may be any that keep to these rules, and one draw needn't show every extreme that they name: `sample_lengths`: in each row, the lengths sum to 640 and one sample has exactly 128 live tokens.
All inputs are finite; a program needn't handle non-finite values.
Results may differ from a plain program's by a relative error of at most 0.0047.
Values may be sent and summed in bfloat16 or wider, within the bound.
A program may use at most 128 MiB of HBM per device.

v0:
```python
import jax
import jax.numpy as jnp
from jax import lax
from jax.sharding import PartitionSpec as P

D = 8192
SLOT = 128


def slot_lengths(slot_ids, flat, sample_count):
    sample_ids = jnp.arange(sample_count, dtype=jnp.int32)
    return jnp.sum(jnp.where(slot_ids[:, None] == sample_ids[None, :], flat[None, :], 0), axis=1)


def shards(tokens, gate_weight, up_weight, down_frozen, down_learn, steer, sample_lengths):
    rows_tp = tokens.shape[0]
    cols = tokens.shape[1]
    width_ff = gate_weight.shape[1]
    n_tensor = lax.axis_size("tensor")
    total_rows = rows_tp * n_tensor
    seq_count = sample_lengths.shape[1]
    flat = sample_lengths.reshape(-1)
    gathered = lax.all_gather(tokens, "tensor", axis=0, tiled=True)
    source_ids = jnp.arange(total_rows, dtype=jnp.int32)
    count_rows = gathered.shape[0]
    both_in = jnp.concatenate([gate_weight, up_weight], axis=1)
    block = gathered
    summed = lax.psum_scatter(
        jnp.dot(block, both_in, preferred_element_type=jnp.float32),
        "fsdp",
        scatter_dimension=0,
        tiled=True,
    )
    hidden_own = (jax.nn.silu(summed[:, :width_ff]) * summed[:, width_ff:]).astype(jnp.bfloat16)
    hidden_all = lax.all_gather(hidden_own, "fsdp", axis=0, tiled=True)
    both_out = jnp.concatenate([down_frozen, down_learn], axis=1)
    own_count = count_rows // n_tensor
    block = hidden_all
    mlp_terms = lax.psum_scatter(
        jnp.dot(block, both_out, preferred_element_type=jnp.float32),
        "tensor",
        scatter_dimension=0,
        tiled=True,
    )
    own_start = lax.axis_index("tensor") * own_count
    base = lax.dynamic_slice_in_dim(gathered, own_start, own_count, 0).astype(jnp.float32)
    out_frozen = base + mlp_terms[:, :cols]
    out_learn = base + mlp_terms[:, cols:]
    row_ids = lax.dynamic_slice_in_dim(source_ids, own_start, own_count, 0)
    row_len = slot_lengths(row_ids // SLOT, flat, 2 * seq_count)
    live = row_ids % SLOT < row_len
    forget = (live & (row_ids < seq_count * SLOT))[:, None]
    retain = (live & (row_ids >= seq_count * SLOT))[:, None]
    scale = 20.0 / jnp.sqrt(D * (jnp.mean(steer * steer) + 1e-06))
    target = scale * lax.dynamic_slice_in_dim(steer, lax.axis_index("fsdp") * cols, cols)
    steer_diff = out_learn - target[None, :]
    keep_diff = out_learn - out_frozen
    zero = jnp.zeros((), jnp.float32)
    local_steer = jnp.sum(jnp.where(forget, steer_diff * steer_diff, zero))
    local_keep = jnp.sum(jnp.where(retain, keep_diff * keep_diff, zero))
    sum_steer, sum_keep = lax.psum((local_steer, local_keep), ("fsdp", "tensor"))
    count_f = jnp.sum(sample_lengths[0]).astype(jnp.float32)
    count_r = jnp.sum(sample_lengths[1]).astype(jnp.float32)
    losses = jnp.stack([sum_steer / (count_f * D), sum_keep / (count_r * D)])
    delta = (jnp.where(forget, steer_diff, zero) + 2.0 * jnp.where(retain, keep_diff, zero)).astype(
        jnp.bfloat16
    )
    delta_all = lax.all_gather(delta, "tensor", axis=0, tiled=True)
    grad_down = lax.dot_general(
        hidden_all, delta_all, (((0,), (0,)), ((), ())), preferred_element_type=jnp.float32
    )
    return (grad_down, losses)


def solution(mesh):
    return jax.shard_map(
        shards,
        mesh=mesh,
        in_specs=(
            P("tensor", "fsdp"),
            P("fsdp", "tensor"),
            P("fsdp", "tensor"),
            P("tensor", "fsdp"),
            P("tensor", "fsdp"),
            P(),
            P(),
        ),
        out_specs=(P("tensor", "fsdp"), P()),
        check_vma=False,
    )
```

profile of v0, /device:TPU:1, one launch (start us, length us, event | category | flops | bytes accessed | tf_op | source)
XLA Modules:
  0.0 669.6 jit_solution(13984277095447534739)
XLA Ops:
  7.2 0.0 all-gather.4.cloned.1.call-start
  7.2 0.7 all-gather.4.cloned.1.call-update
  7.9 0.0 reduce-scatter.3.cloned.1.call-start
  7.9 58.6 %all-gather.4.cloned.1.call-done = bf16[2048,512]{1,0:T(8,128)(2,1)} async-done(((bf16[256,512]{1,0:T(8,128)(2,1)}), bf16[2048,512]{1,0:T(8,128)(2,1)}) %all-gather.4.cloned.1.call-update) | async-done | bytes 2097168 | tf_op jit(solution)/shard_map/all_gather | solution.py:23
  66.6 16.0 %convolution_bitcast_fusion = f32[2048,3584]{0,1:T(8,128)} fusion(bf16[2048,512]{1,0:T(8,128)(2,1)} %all-gather.4.cloned.1.call-done, bf16[512,1792]{1,0:T(8,128)(2,1)} %param.9, bf16[512,1792]{1,0:T(8,128)(2,1)} %param.8), kind=kOutput, calls=%fused_computation | convolution fusion | flops 7523532800 | bytes 35127296 | tf_op jit(solution)/shard_map/dot_general | solution.py:29
  82.6 0.0 copy-start.2
  82.6 0.0 reduce-scatter.3.cloned.1.call-update
  82.6 0.0 all-gather.6.cloned.1.call-start
  82.7 306.2 %reduce-scatter.3.cloned.1.call-done = f32[128,3584]{0,1:T(8,128)} async-done(((f32[2048,3584]{0,1:T(8,128)}), f32[128,3584]{0,1:T(8,128)}) %reduce-scatter.3.cloned.1.call-update) | async-done | bytes 1835024 | tf_op jit(solution)/shard_map/reduce_scatter | solution.py:28
  388.9 2.5 fusion.7
  391.3 0.0 all-gather.6.cloned.1.call-update
  391.4 0.0 reduce-scatter.5.cloned.1.call-start
  391.4 56.4 %all-gather.6.cloned.1.call-done = bf16[2048,1792]{0,1:T(8,128)(2,1)} async-done(((bf16[128,1792]{0,1:T(8,128)(2,1)}), bf16[2048,1792]{0,1:T(8,128)(2,1)}) %all-gather.6.cloned.1.call-update) | async-done | bytes 7340048 | tf_op jit(solution)/shard_map/all_gather | solution.py:35
  447.8 0.0 copy-done.2
  447.8 12.6 %fusion.3 = f32[2048,1024]{1,0:T(8,128)} fusion(bf16[2048,1792]{0,1:T(8,128)(2,1)} %all-gather.6.cloned.1.call-done, bf16[1792,512]{1,0:T(8,128)(2,1)S(1)} %copy-done.2, bf16[1792,512]{1,0:T(8,128)(2,1)} %param.10), kind=kOutput, calls=%fused_computation.4 | convolution fusion | flops 7523532800 | bytes 19398656 | tf_op jit(solution)/shard_map/dot_general | solution.py:40
  460.5 0.0 copy-start
  460.5 0.0 copy-start.1
  460.5 0.0 reduce-scatter.5.cloned.1.call-update
  460.5 0.0 all-gather.8.cloned.1.call-start
  460.5 0.7 copy-done
  461.2 0.6 multiply_reduce_fusion
  462.5 0.0 copy-done.1
  462.5 0.1 broadcast_in_dim.45
  462.6 0.1 dynamic-slice_multiply_fusion
  462.7 0.1 select_reduce_fusion.2
  462.8 111.7 %reduce-scatter.5.cloned.1.call-done = f32[256,1024]{1,0:T(8,128)} async-done(((f32[2048,1024]{1,0:T(8,128)}), f32[256,1024]{1,0:T(8,128)}) %reduce-scatter.5.cloned.1.call-update) | async-done | bytes 1048592 | tf_op jit(solution)/shard_map/reduce_scatter | solution.py:39
  574.5 2.8 select_reduce_fusion.1
  577.4 0.0 all-gather.8.cloned.1.call-update
  577.4 0.7 slice_reduce_fusion.1
  579.3 72.4 %all-reduce = (f32[]{:T(128)}, f32[]{:T(128)}) all-reduce(f32[]{:T(128)} %get-tuple-element.3, f32[]{:T(128)} %get-tuple-element.2), channel_id=1, replica_groups=mesh['fsdp'=16,'tensor'=8] {'fsdp','tensor'}, use_global_device_ids=true, to_apply=%region_8.9 | all-reduce | flops 2 | bytes 16 | tf_op jit(solution)/shard_map/psum | solution.py:61
  653.0 0.6 pad_maximum_fusion
  653.6 9.5 %fusion.15 = f32[1792,512]{1,0:T(8,128)} fusion(bf16[2048,1792]{0,1:T(8,128)(2,1)} %all-gather.6.cloned.1.call-done, bf16[2048,512]{1,0:T(8,128)(2,1)} %all-gather.8.cloned.1.call-done), kind=kOutput, calls=%fused_computation.37 | convolution fusion | flops 3758096384 | bytes 13107200 | tf_op jit(solution)/shard_map/dot_general | solution.py:69
  (4 shorter events, 0.0 us)
Async XLA Ops:
  7.2 59.4 %all-gather.4.cloned.1.call-start = ((), (), s32[]{:S(2)}) async-start(), calls=%async_computation.2 | async-start | bytes 2359296 | tf_op jit(solution)/shard_map/all_gather | solution.py:23
  7.9 381.0 %reduce-scatter.3.cloned.1.call-start = ((), (), s32[]{:S(2)}) async-start(), calls=%async_computation.3 | async-start | bytes 31195136 | tf_op jit(solution)/shard_map/reduce_scatter | solution.py:28
  82.6 365.2 %copy-start.2 = (bf16[1792,512]{1,0:T(8,128)(2,1)S(1)}, bf16[1792,512]{1,0:T(8,128)(2,1)}, u32[]{:S(2)}) copy-start(bf16[1792,512]{1,0:T(8,128)(2,1)} %param.11) | copy-start | bytes 5505028
  82.6 365.2 %all-gather.6.cloned.1.call-start = ((), (), s32[]{:S(2)}) async-start(), calls=%async_computation.4 | async-start | bytes 7798784 | tf_op jit(solution)/shard_map/all_gather | solution.py:35
  391.4 183.2 %reduce-scatter.5.cloned.1.call-start = ((), (), s32[]{:S(2)}) async-start(), calls=%async_computation.5 | async-start | bytes 9437184 | tf_op jit(solution)/shard_map/reduce_scatter | solution.py:39
  460.5 0.8 copy-start
  460.5 2.1 copy-start.1
  460.5 193.1 %all-gather.8.cloned.1.call-start = ((), (), s32[]{:S(2)}) async-start(), calls=%async_computation.6 | async-start | bytes 2359296 | tf_op jit(solution)/shard_map/all_gather | solution.py:68
Sparse Core Ops, SparseCore 0:
  10.3 56.1 all-gather.3
  82.7 306.0 reduce-scatter.2
  391.5 56.3 all-gather.5
  460.6 113.8 reduce-scatter.4
  577.5 51.8 all-gather.7
where the time goes:
time: 670 us
  waiting for transfers between devices  534 us (80%)
  blocking collectives  72.4 us (11%)
  matrix products  38.1 us (6%)
  between operations  17 us (3%)
  other arithmetic  7.37 us (1%)
    reduce_scatter x1, waiting for transfers between devices, shards(): lax.psum_scatter(jnp.dot(block, both_in, preferred_element_type=jnp.float...  306 us
    reduce_scatter x1, waiting for transfers between devices, shards(): lax.psum_scatter(jnp.dot(block, both_out, preferred_element_type=jnp.floa...  112 us
    psum x1, blocking collectives, shards(): lax.psum((local_steer, local_keep), ('fsdp', 'tensor'))  72.4 us
    all_gather x1, waiting for transfers between devices, shards(): gathered = lax.all_gather(tokens, 'tensor', axis=0, tiled=True)  58.6 us
    all_gather x1, waiting for transfers between devices, shards(): hidden_all = lax.all_gather(hidden_own, 'fsdp', axis=0, tiled=True)  56.4 us
    dot_general x1, matrix products, shards(): jnp.dot(block, both_in, preferred_element_type=jnp.float32)  16 us
  transfers between devices with their start and end apart: 5, of which 4 were waited for; matrix products, arithmetic and copies ran while one was open for 0% of the time, Pallas kernels for 0%

commit v1 on v0

v1 whole, which is shorter than its diff:
```python
import jax
import jax.numpy as jnp
from jax import lax
from jax.experimental import pallas as pl
from jax.experimental.pallas import tpu as pltpu
from jax.sharding import PartitionSpec as P

MESH = pl.DeviceIdType.MESH
BF16 = jnp.bfloat16
F32 = jnp.float32

D = 8192
SLOT = 128
SEQS = 8
HALF = 640
RAW = 1024
NF = 8
NT = 8
CH = HALF // NF
W = 512
FF = 1792
HF = FF // 2
TN = 256


def encode(v):
    return (v * jnp.abs(v)).astype(BF16)


def decode(t):
    t = t.astype(F32)
    return t * lax.rsqrt(jnp.maximum(jnp.abs(t), 1.2e-38))


def kernel(
    lens, steer, tok_in, gw, uw, wf_in, wl_in,
    hid_out, delta_out, loss_out,
    tok, ctok, wts, send, recv, hid, wf, wl, dsend, drecv, delta, loss, lrecv,
    tz_s, tz_r, ty_s, ty_r, loc, w_s, w_r, c_s, c_r, rs_s, rs_r, ag_s, ag_r, pr_s, pr_r,
    ds_s, ds_r, dg_s, dg_r, ls_s, ls_r, out_sem,
):
    f = lax.axis_index("fsdp")
    t = lax.axis_index("tensor")
    c = f % 2
    q = f // 2
    x = f // 4
    yl = q % 2
    yh = t // 4
    z = t % 4
    partner = f + 1 - 2 * c

    def fpeer(k, sign=1):
        dx, dy = k // 2, k % 2
        return ((x + 4 + sign * dx) % 4) * 2 + (yl + dy) % 2

    def tpeer(k, sign=1):
        dy, dz = k // 4, k % 4
        return ((yh + dy) % 2) * 4 + (z + 4 + sign * dz) % 4

    def rcopy(src, dst, ss, rs, to_f, to_t):
        return pltpu.make_async_remote_copy(
            src_ref=src, dst_ref=dst, send_sem=ss, recv_sem=rs,
            device_id=(to_f, to_t), device_id_type=MESH,
        )

    mine_c = pl.ds(pl.multiple_of(c * W, W), W)
    rows_t = lambda s: pl.ds(pl.multiple_of(s * 256, 256), 256)
    my_cols = pl.ds(pl.multiple_of(c * HF, HF), HF)
    other_cols = pl.ds(pl.multiple_of((1 - c) * HF, HF), HF)
    rows_w = pl.ds(pl.multiple_of(c * W, W), W)
    own_tok = pltpu.make_async_copy(tok_in, tok.at[rows_t(t)], loc.at[0])
    own_tok.start()
    local = [
        pltpu.make_async_copy(gw.at[:, my_cols], wts.at[rows_w, pl.ds(0, HF)], loc.at[1]),
        pltpu.make_async_copy(uw.at[:, my_cols], wts.at[rows_w, pl.ds(HF, HF)], loc.at[2]),
        pltpu.make_async_copy(wl_in, wl, loc.at[3]),
        pltpu.make_async_copy(wf_in, wf, loc.at[4]),
    ]
    for cp in local:
        cp.start()

    barrier = pltpu.get_barrier_semaphore()
    for k in range(1, NF):
        pl.semaphore_signal(barrier, inc=1, device_id=(fpeer(k) * 2 + c, t), device_id_type=MESH)
        pl.semaphore_signal(barrier, inc=1, device_id=(f, tpeer(k)), device_id_type=MESH)
    pl.semaphore_signal(barrier, inc=1, device_id=(partner, t), device_id_type=MESH)
    pl.semaphore_wait(barrier, 15)

    sends = []

    def go(cp):
        cp.start()
        sends.append(cp)

    yo = (1 - yh) * 4 + z
    go(rcopy(tok_in, tok.at[rows_t(t)], ty_s, ty_r, f, yo))
    for dz in range(1, 4):
        go(rcopy(tok_in, tok.at[rows_t(t)], tz_s.at[0, dz - 1], tz_r.at[0, dz - 1], f, tpeer(dz)))
    go(rcopy(gw.at[:, other_cols], wts.at[rows_w, pl.ds(0, HF)], w_s.at[0], w_r.at[0], partner, t))
    go(rcopy(uw.at[:, other_cols], wts.at[rows_w, pl.ds(HF, HF)], w_s.at[1], w_r.at[1], partner, t))

    rcopy(tok_in, tok.at[rows_t(yo)], ty_s, ty_r, f, yo).wait_recv()
    for dz in range(1, 4):
        go(rcopy(tok.at[rows_t(yo)], tok.at[rows_t(yo)], tz_s.at[1, dz - 1], tz_r.at[1, dz - 1], f, tpeer(dz)))
    own_tok.wait()
    for g in range(2):
        for dz in range(1, 4):
            s = tpeer(dz + 4 * g, -1)
            rcopy(tok_in, tok.at[rows_t(s)], tz_s.at[g, dz - 1], tz_r.at[g, dz - 1], f, s).wait_recv()

    rid = lax.broadcasted_iota(jnp.int32, (HALF, SLOT), 0)
    lane = lax.broadcasted_iota(jnp.int32, (HALF, SLOT), 1)
    for h in range(2):
        off = jnp.int32(0)
        total = jnp.zeros((HALF, W), F32)
        picks = []
        for k in range(SEQS):
            n = lens[h, k]
            picks.append(jnp.where((rid == off + lane) & (lane < n), 1.0, 0.0).astype(BF16))
            off = off + n
        pick = jnp.concatenate(picks, axis=1)
        hr = pl.ds(h * HALF, HALF)
        ctok[hr, mine_c] = jnp.dot(
            pick, tok[pl.ds(h * RAW, RAW), :], preferred_element_type=F32
        ).astype(BF16)
        go(rcopy(ctok.at[hr, mine_c], ctok.at[hr, mine_c], c_s.at[h], c_r.at[h], partner, t))

    for cp in local:
        cp.wait()
    his_rows = pl.ds(pl.multiple_of((1 - c) * W, W), W)
    rcopy(gw.at[:, other_cols], wts.at[his_rows, pl.ds(0, HF)], w_s.at[0], w_r.at[0], partner, t).wait_recv()
    rcopy(uw.at[:, other_cols], wts.at[his_rows, pl.ds(HF, HF)], w_s.at[1], w_r.at[1], partner, t).wait_recv()

    own_rows = lambda h, who: pl.ds(pl.multiple_of(h * HALF + who * CH, CH), CH)
    for h in range(2):
        hr = pl.ds(h * HALF, HALF)
        rcopy(ctok.at[hr, mine_c], ctok.at[hr, his_rows], c_s.at[h], c_r.at[h], partner, t).wait_recv()

        def tile(n, carry):
            cols = pl.ds(pl.multiple_of(n * TN, TN), TN)
            send[hr, cols] = encode(jnp.dot(ctok[hr, :], wts[:, cols], preferred_element_type=F32))
            return carry

        lax.fori_loop(0, FF // TN, tile, 0)
        for k in range(1, NF):
            p = fpeer(k)
            go(rcopy(send.at[own_rows(h, p)], recv.at[h, k - 1], rs_s.at[h, k - 1], rs_r.at[h, k - 1], p * 2 + c, t))

    def reduce_hidden(h):
        for k in range(1, NF):
            p = fpeer(k)
            rcopy(send.at[own_rows(h, p)], recv.at[h, k - 1], rs_s.at[h, k - 1], rs_r.at[h, k - 1], p * 2 + c, t).wait_recv()
        mine = own_rows(h, q)

        def tile(j, carry):
            gc = pl.ds(pl.multiple_of(j * 128, 128), 128)
            uc = pl.ds(pl.multiple_of(HF + j * 128, 128), 128)
            gate = decode(send[mine, gc])
            up = decode(send[mine, uc])
            for k in range(NF - 1):
                gate += decode(recv[h, k, :, gc])
                up += decode(recv[h, k, :, uc])
            value = (gate * jax.nn.sigmoid(gate) * up).astype(BF16)
            hid[mine, pl.ds(pl.multiple_of(c * HF + j * 128, 128), 128)] = value
            return carry

        lax.fori_loop(0, HF // 128, tile, 0)
        for k in range(1, NF):
            p = fpeer(k)
            go(rcopy(hid.at[mine, my_cols], hid.at[mine, my_cols], ag_s.at[h, k - 1], ag_r.at[h, k - 1], p * 2 + c, t))

    def relay_hidden(h):
        for k in range(1, NF):
            p = fpeer(k, -1)
            region = hid.at[own_rows(h, p), my_cols]
            rcopy(region, region, ag_s.at[h, k - 1], ag_r.at[h, k - 1], p * 2 + c, t).wait_recv()
        region = hid.at[pl.ds(h * HALF, HALF), my_cols]
        go(rcopy(region, region, pr_s.at[h], pr_r.at[h], partner, t))

    outs = []

    def down(h):
        region = hid.at[pl.ds(h * HALF, HALF), other_cols]
        rcopy(region, region, pr_s.at[h], pr_r.at[h], partner, t).wait_recv()
        hr = pl.ds(h * HALF, HALF)
        cp = pltpu.make_async_copy(hid.at[hr], hid_out.at[hr], out_sem.at[h])
        cp.start()
        outs.append(cp)

        def tile(n, carry):
            cols = pl.ds(pl.multiple_of(n * TN, TN), TN)
            acc = jnp.dot(hid[hr, :], wl[:, cols], preferred_element_type=F32)
            if h == 1:
                acc = acc - jnp.dot(hid[hr, :], wf[:, cols], preferred_element_type=F32)
            dsend[hr, cols] = encode(acc)
            return carry

        lax.fori_loop(0, W // TN, tile, 0)
        for k in range(1, NT):
            p = tpeer(k)
            go(rcopy(dsend.at[own_rows(h, p)], drecv.at[h, k - 1], ds_s.at[h, k - 1], ds_r.at[h, k - 1], f, p))

    def make_delta(h):
        for k in range(1, NT):
            p = tpeer(k)
            rcopy(dsend.at[own_rows(h, p)], drecv.at[h, k - 1], ds_s.at[h, k - 1], ds_r.at[h, k - 1], f, p).wait_recv()
        mine = own_rows(h, t)
        value = decode(dsend[mine, :])
        for k in range(NT - 1):
            value += decode(drecv[h, k])
        if h == 0:
            st = steer[...]
            mean = jnp.sum(st * st, keepdims=True) * (1.0 / D)
            scale = 20.0 / jnp.sqrt(D * (mean + 1e-06))
            diff = ctok[mine, mine_c].astype(F32) + value - steer[pl.ds(f, 1), :] * scale
            out = diff
        else:
            diff = value
            out = 2.0 * value
        loss[0, h] = jnp.broadcast_to(jnp.sum(diff * diff, keepdims=True), (8, 128))
        delta[mine, :] = out.astype(BF16)
        for k in range(1, NT):
            go(rcopy(delta.at[mine], delta.at[mine], dg_s.at[h, k - 1], dg_r.at[h, k - 1], f, tpeer(k)))

    def get_delta(h):
        for k in range(1, NT):
            p = tpeer(k, -1)
            region = delta.at[own_rows(h, p)]
            rcopy(region, region, dg_s.at[h, k - 1], dg_r.at[h, k - 1], f, p).wait_recv()
        hr = pl.ds(h * HALF, HALF)
        cp = pltpu.make_async_copy(delta.at[hr], delta_out.at[hr], out_sem.at[2 + h])
        cp.start()
        outs.append(cp)

    reduce_hidden(0)
    reduce_hidden(1)
    relay_hidden(0)
    down(0)
    relay_hidden(1)
    down(1)
    make_delta(0)
    make_delta(1)

    def share(stage, peers):
        waits = []
        for i, (pf, pt) in enumerate(peers):
            slot = 7 * stage + i
            cp = rcopy(loss.at[stage], lrecv.at[slot], ls_s.at[slot], ls_r.at[slot], pf, pt)
            go(cp)
            waits.append(cp)
        for cp in waits:
            cp.wait_recv()
        value = loss[stage]
        for i in range(len(peers)):
            value = value + lrecv[7 * stage + i]
        loss[stage + 1] = value

    share(0, [(f, tpeer(k)) for k in range(1, NT)])
    share(1, [(fpeer(k) * 2 + c, t) for k in range(1, NF)])
    share(2, [(partner, t)])
    loss_out[...] = loss[3]

    get_delta(0)
    get_delta(1)
    for cp in sends:
        cp.wait_send()
    for cp in outs:
        cp.wait()


def shards(tokens, gate_weight, up_weight, down_frozen, down_learn, steer, sample_lengths):
    any_spec = pl.BlockSpec(memory_space=pl.ANY)
    vmem = pltpu.VMEM
    dma = pltpu.SemaphoreType.DMA
    rows = 2 * HALF
    hid, delta, sums = pl.pallas_call(
        kernel,
        out_shape=(
            jax.ShapeDtypeStruct((rows, FF), BF16),
            jax.ShapeDtypeStruct((rows, W), BF16),
            jax.ShapeDtypeStruct((2, 8, 128), F32),
        ),
        in_specs=[
            pl.BlockSpec(memory_space=pltpu.SMEM),
            pl.BlockSpec(memory_space=pltpu.VMEM),
        ] + [any_spec] * 5,
        out_specs=(any_spec, any_spec, pl.BlockSpec(memory_space=pltpu.VMEM)),
        scratch_shapes=[
            vmem((2 * RAW, W), BF16),
            vmem((rows, 2 * W), BF16),
            vmem((2 * W, FF), BF16),
            vmem((rows, FF), BF16),
            vmem((2, NF - 1, CH, FF), BF16),
            vmem((rows, FF), BF16),
            vmem((FF, W), BF16),
            vmem((FF, W), BF16),
            vmem((rows, W), BF16),
            vmem((2, NT - 1, CH, W), BF16),
            vmem((rows, W), BF16),
            vmem((4, 2, 8, 128), F32),
            vmem((15, 2, 8, 128), F32),
            dma((2, 3)), dma((2, 3)), dma, dma, dma((5,)),
            dma((2,)), dma((2,)), dma((2,)), dma((2,)),
            dma((2, 7)), dma((2, 7)), dma((2, 7)), dma((2, 7)), dma((2,)), dma((2,)),
            dma((2, 7)), dma((2, 7)), dma((2, 7)), dma((2, 7)), dma((15,)), dma((15,)),
            dma((4,)),
        ],
        compiler_params=pltpu.CompilerParams(
            collective_id=0, has_side_effects=True, vmem_limit_bytes=60 * 1024 * 1024
        ),
    )(sample_lengths, steer.reshape(16, W), tokens, gate_weight, up_weight, down_frozen, down_learn)
    grad_down = lax.dot_general(hid, delta, (((0,), (0,)), ((), ())), preferred_element_type=F32)
    counts = jnp.sum(sample_lengths, axis=1).astype(F32)
    losses = sums[:, 0, 0] / (counts * D)
    return (grad_down, losses)


def solution(mesh):
    return jax.shard_map(
        shards,
        mesh=mesh,
        in_specs=(
            P("tensor", "fsdp"),
            P("fsdp", "tensor"),
            P("fsdp", "tensor"),
            P("tensor", "fsdp"),
            P("tensor", "fsdp"),
            P(),
            P(),
        ),
        out_specs=(P("tensor", "fsdp"), P()),
        check_vma=False,
    )
```

time: 670 us -> 188 us (0.28)
  waiting for transfers between devices: 534 us -> 0 us
  Pallas kernels: 0 us -> 177 us
  blocking collectives: 72.4 us -> 0 us
  matrix products: 38.1 us -> 7.12 us
  between operations: 17 us -> 0.65 us
  other arithmetic: 7.37 us -> 0.64 us
    reduce_scatter x2 -> x0, waiting for transfers between devices: 418 us -> none  [the longest x1 306 us: shards(): lax.psum_scatter(jnp.dot(block, both_in, preferred_element_type=jnp.float...]
    pallas_call x0 -> x1, Pallas kernels: none -> 177 us  [shards(): pl.pallas_call(kernel, out_shape=(jax.ShapeDtypeStruct((rows, FF), BF16),...]
    all_gather x3 -> x0, waiting for transfers between devices: 115 us -> none  [the longest x1 58.6 us: shards(): gathered = lax.all_gather(tokens, 'tensor', axis=0, tiled=True)]
    psum x1 -> x0, blocking collectives: 72.4 us -> none  [shards(): lax.psum((local_steer, local_keep), ('fsdp', 'tensor'))]
    dot_general x3 -> x1, matrix products: 38.1 us -> 7.12 us  [shards(): lax.dot_general(hid, delta, (((0,), (0,)), ((), ())), preferred_element_t...]
  transfers between devices with their start and end apart: 5 -> 0, of which waited for: 4 -> 0; matrix products, arithmetic and copies ran while one was open for 0% -> 0% of each run, Pallas kernels for 0% -> 0%
where the time goes in v1:
time: 188 us
  Pallas kernels  177 us (94%)
  matrix products  7.12 us (4%)
  local copies, waits for them, and re-layouts  2.18 us (1%)
    pallas_call x1, Pallas kernels, shards(): pl.pallas_call(kernel, out_shape=(jax.ShapeDtypeStruct((rows, FF), BF16),...  177 us
    dot_general x1, matrix products, shards(): lax.dot_general(hid, delta, (((0,), (0,)), ((), ())), preferred_element_t...  7.12 us

profile of v1, /device:TPU:1, one launch (start us, length us, event | category | flops | bytes accessed | tf_op | source)
XLA Modules:
  0.0 188.0 jit_solution(10099687295134733363)
XLA Ops:
  0.6 1.4 reshape.7.steer
  2.0 177.4 %shard_map.86 = (bf16[1280,1792]{1,0:T(8,128)(2,1)}, bf16[1280,512]{1,0:T(8,128)(2,1)}, f32[2,8,128]{2,1,0:T(8,128)}) custom-call(s32[2,8]{1,0:T(2,128)} %lens.1, f32[16,512]{1,0:T(8,128)} %reshape.7.steer, bf16[256,512]{1,0:T(8,128)(2,1)} %tok_in.1, bf16[512,1792]{1,0:T(8,128)(2,1)} %gw.1, bf16[512,1792]{1,0:T(8,128)(2,1)} %uw.1, bf16[1792,512]{1,0:T(8,128)(2,1)} %wf_in.1, ...), custom_call_target="tpu_custom_call" | custom-call | tf_op jit(solution)/shard_map/pallas_call | solution.py:276
  179.4 0.0 copy-start
  179.4 7.1 %fusion = f32[1792,512]{1,0:T(8,128)} fusion(bf16[1280,1792]{1,0:T(8,128)(2,1)} %get-tuple-element.5, bf16[1280,512]{1,0:T(8,128)(2,1)} %get-tuple-element.6), kind=kOutput, calls=%fused_computation.2 | convolution fusion | flops 2348810240 | bytes 9568256 | tf_op jit(solution)/shard_map/dot_general | solution.py:312
  186.5 0.8 slice_reduce_fusion
  187.3 0.0 copy-done
  187.3 0.1 reduce_sum.9
  187.4 0.5 multiply_divide_fusion
Async XLA Ops:
  179.4 7.9 %copy-start = (s32[2,8]{1,0:T(2,128)S(1)}, s32[2,8]{1,0:T(2,128)}, u32[]{:S(2)}) copy-start(s32[2,8]{1,0:T(2,128)} %lens.1) | copy-start | bytes 196

commit v2 on v1

v2 whole, which is shorter than its diff:
```python
import jax
import jax.numpy as jnp
from jax import lax
from jax.experimental import pallas as pl
from jax.experimental.pallas import tpu as pltpu
from jax.sharding import PartitionSpec as P

MESH = pl.DeviceIdType.MESH
BF16 = jnp.bfloat16
F32 = jnp.float32

D = 8192
SLOT = 128
SEQS = 8
HALF = 640
RAW = 1024
NF = 8
NT = 8
W = 512
FF = 1792
HF = FF // 2
TN = 256


def encode(v):
    return (v * jnp.abs(v)).astype(BF16)


def decode(t):
    t = t.astype(F32)
    return t * lax.rsqrt(jnp.maximum(jnp.abs(t), 1.2e-38))


CHUNKS = ((0, 48), (0, 48), (1, 32), (1, 32))
PART0 = 384


def kernel(
    lens, steer, tok_in, gw, uw, wf_in, wl_in,
    grad_out, loss_out,
    tok, ctok, wts, send, recv, hid, wf, wl, acc, dsend, drecv, delta, grad, loss, lrecv,
    tz_s, tz_r, ty_s, ty_r, loc, w_s, w_r, c_s, c_r, rs_s, rs_r, ag_s, ag_r, pr_s, pr_r,
    ds_s, ds_r, dg_s, dg_r, ls_s, ls_r, out_sem,
):
    f = lax.axis_index("fsdp")
    t = lax.axis_index("tensor")
    c = f % 2
    q = f // 2
    x = f // 4
    yl = q % 2
    yh = t // 4
    z = t % 4
    partner = f + 1 - 2 * c

    def fpeer(k, sign=1):
        dx, dy = k // 2, k % 2
        return ((x + 4 + sign * dx) % 4) * 2 + (yl + dy) % 2

    def tpeer(k, sign=1):
        dy, dz = k // 4, k % 4
        return ((yh + dy) % 2) * 4 + (z + 4 + sign * dz) % 4

    def rcopy(src, dst, ss, rs, to_f, to_t):
        return pltpu.make_async_remote_copy(
            src_ref=src, dst_ref=dst, send_sem=ss, recv_sem=rs,
            device_id=(to_f, to_t), device_id_type=MESH,
        )

    def at(start, size, step=16):
        return pl.ds(pl.multiple_of(start, step), size)

    mine_c = at(c * W, W, W)
    his_c = at((1 - c) * W, W, W)
    my_cols = at(c * HF, HF, 128)
    other_cols = at((1 - c) * HF, HF, 128)
    rows_t = lambda s: at(s * 256, 256, 256)

    own_tok = pltpu.make_async_copy(tok_in, tok.at[rows_t(t)], loc.at[0])
    own_tok.start()
    local = [
        pltpu.make_async_copy(gw.at[:, my_cols], wts.at[mine_c, pl.ds(0, HF)], loc.at[1]),
        pltpu.make_async_copy(uw.at[:, my_cols], wts.at[mine_c, pl.ds(HF, HF)], loc.at[2]),
        pltpu.make_async_copy(wl_in, wl, loc.at[3]),
        pltpu.make_async_copy(wf_in, wf, loc.at[4]),
    ]
    for cp in local:
        cp.start()

    barrier = pltpu.get_barrier_semaphore()
    for k in range(1, NF):
        pl.semaphore_signal(barrier, inc=1, device_id=(fpeer(k) * 2 + c, t), device_id_type=MESH)
        pl.semaphore_signal(barrier, inc=1, device_id=(f, tpeer(k)), device_id_type=MESH)
    pl.semaphore_signal(barrier, inc=1, device_id=(partner, t), device_id_type=MESH)
    pl.semaphore_wait(barrier, 15)

    sends = []
    outs = []

    def go(cp):
        cp.start()
        sends.append(cp)

    yo = (1 - yh) * 4 + z
    go(rcopy(tok_in, tok.at[rows_t(t)], ty_s, ty_r, f, yo))
    for dz in range(1, 4):
        go(rcopy(tok_in, tok.at[rows_t(t)], tz_s.at[0, dz - 1], tz_r.at[0, dz - 1], f, tpeer(dz)))
    go(rcopy(gw.at[:, other_cols], wts.at[mine_c, pl.ds(0, HF)], w_s.at[0], w_r.at[0], partner, t))
    go(rcopy(uw.at[:, other_cols], wts.at[mine_c, pl.ds(HF, HF)], w_s.at[1], w_r.at[1], partner, t))

    kinds = (yh, 1 - yh, 0, 1)
    ids = (yh, 1 - yh, 2, 3)
    base_of = lambda kind, part: kind * HALF + part * PART0

    def rows_of(kind, part, start, size):
        return at(base_of(kind, part) + start, size)

    def compact(i):
        kind = kinds[i]
        for dz in range(1, 4):
            s = tpeer(dz + 4 * i, -1)
            rcopy(tok_in, tok.at[rows_t(s)], tz_s.at[i, dz - 1], tz_r.at[i, dz - 1], f, s).wait_recv()
        rid = lax.broadcasted_iota(jnp.int32, (HALF, SLOT), 0)
        lane = lax.broadcasted_iota(jnp.int32, (HALF, SLOT), 1)
        off = jnp.int32(0)
        picks = []
        for k in range(SEQS):
            n = jnp.where(kind == 0, lens[0, k], lens[1, k])
            picks.append(jnp.where((rid == off + lane) & (lane < n), 1.0, 0.0).astype(BF16))
            off = off + n
        hr = at(kind * HALF, HALF)
        ctok[hr, mine_c] = jnp.dot(
            jnp.concatenate(picks, axis=1), tok[at(kind * RAW, RAW), :], preferred_element_type=F32
        ).astype(BF16)
        go(rcopy(ctok.at[hr, mine_c], ctok.at[hr, mine_c], c_s.at[i], c_r.at[i], partner, t))

    def from_partner(i):
        hr = at(kinds[i] * HALF, HALF)
        rcopy(ctok.at[hr, mine_c], ctok.at[hr, his_c], c_s.at[i], c_r.at[i], partner, t).wait_recv()

    def gate_up(p):
        part, n = CHUNKS[p]
        rows = rows_of(kinds[p], part, 0, NF * n)

        def tile(j, carry):
            cols = at(j * TN, TN, TN)
            send[rows, cols] = encode(jnp.dot(ctok[rows, :], wts[:, cols], preferred_element_type=F32))
            return carry

        lax.fori_loop(0, FF // TN, tile, 0)

    def rs_copy(p, k):
        part, n = CHUNKS[p]
        to = fpeer(k)
        return rcopy(
            send.at[rows_of(kinds[p], part, to * n, n)], recv.at[p, k - 1, pl.ds(0, n)],
            rs_s.at[p, k - 1], rs_r.at[p, k - 1], to * 2 + c, t,
        )

    def scatter_hidden(p):
        for k in range(1, NF):
            go(rs_copy(p, k))

    def reduce_hidden(p):
        for k in range(1, NF):
            rs_copy(p, k).wait_recv()
        part, n = CHUNKS[p]
        mine = rows_of(kinds[p], part, q * n, n)

        def tile(j, carry):
            gc = at(j * 128, 128, 128)
            uc = at(HF + j * 128, 128, 128)
            gate = decode(send[mine, gc])
            up = decode(send[mine, uc])
            for k in range(NF - 1):
                gate += decode(recv[p, k, pl.ds(0, n), gc])
                up += decode(recv[p, k, pl.ds(0, n), uc])
            hid[mine, at(c * HF + j * 128, 128, 128)] = (gate * jax.nn.sigmoid(gate) * up).astype(BF16)
            return carry

        lax.fori_loop(0, HF // 128, tile, 0)
        for k in range(1, NF):
            region = hid.at[mine, my_cols]
            go(rcopy(region, region, ag_s.at[p, k - 1], ag_r.at[p, k - 1], fpeer(k) * 2 + c, t))

    def ds_copy(g, kind, part, n, k):
        to = tpeer(k)
        return rcopy(
            dsend.at[rows_of(kind, part, to * n, n)], drecv.at[g, k - 1, pl.ds(0, n)],
            ds_s.at[g, k - 1], ds_r.at[g, k - 1], f, to,
        )

    def down(p):
        part, n = CHUNKS[p]
        kind, g = kinds[p], ids[p]
        for k in range(1, NF):
            region = hid.at[rows_of(kind, part, fpeer(k, -1) * n, n), my_cols]
            rcopy(region, region, ag_s.at[p, k - 1], ag_r.at[p, k - 1], fpeer(k) * 2 + c, t).wait_recv()
        rows = rows_of(kind, part, 0, NF * n)
        go(rcopy(hid.at[rows, my_cols], hid.at[rows, my_cols], pr_s.at[p], pr_r.at[p], partner, t))

        def product(contract, cols):
            value = jnp.dot(hid[rows, contract], wl[contract, cols], preferred_element_type=F32)
            if p == 2:
                return value
            other = jnp.dot(hid[rows, contract], wf[contract, cols], preferred_element_type=F32)
            if p == 3:
                return value - other
            return value - jnp.where(kind == 1, other, 0.0)

        def first(j, carry):
            cols = at(j * TN, TN, TN)
            acc[pl.ds(0, NF * n), cols] = product(my_cols, cols)
            return carry

        def second(j, carry):
            cols = at(j * TN, TN, TN)
            dsend[rows, cols] = encode(acc[pl.ds(0, NF * n), cols] + product(other_cols, cols))
            return carry

        lax.fori_loop(0, W // TN, first, 0)
        region = hid.at[rows, other_cols]
        rcopy(region, region, pr_s.at[p], pr_r.at[p], partner, t).wait_recv()
        lax.fori_loop(0, W // TN, second, 0)
        for k in range(1, NT):
            go(ds_copy(g, kind, part, n, k))

    def make_delta(g):
        kind = g % 2
        part, n = CHUNKS[g]
        for k in range(1, NT):
            ds_copy(g, kind, part, n, k).wait_recv()
        mine = rows_of(kind, part, t * n, n)
        value = decode(dsend[mine, :])
        for k in range(NT - 1):
            value += decode(drecv[g, k, pl.ds(0, n)])
        if kind == 0:
            st = steer[...]
            mean = jnp.sum(st * st, keepdims=True) * (1.0 / D)
            scale = 20.0 / jnp.sqrt(D * (mean + 1e-06))
            row = jnp.concatenate([steer[pl.ds(f * 4 + i, 1), :] for i in range(4)], axis=1)
            diff = ctok[mine, mine_c].astype(F32) + value - row * scale
            delta[mine, :] = diff.astype(BF16)
        else:
            diff = value
            delta[mine, :] = (2.0 * value).astype(BF16)
        square = jnp.broadcast_to(jnp.sum(diff * diff, keepdims=True), (8, 128))
        loss[0, kind] = square if part == 0 else loss[0, kind] + square
        for k in range(1, NT):
            go(rcopy(delta.at[mine], delta.at[mine], dg_s.at[g, k - 1], dg_r.at[g, k - 1], f, tpeer(k)))

    def add_grad(g):
        kind = g % 2
        part, n = CHUNKS[g]
        for k in range(1, NT):
            who = tpeer(k, -1)
            region = delta.at[rows_of(kind, part, who * n, n)]
            rcopy(region, region, dg_s.at[g, k - 1], dg_r.at[g, k - 1], f, who).wait_recv()
        rows = rows_of(kind, part, 0, NF * n)

        def tile(j, carry):
            cols = at(j * TN, TN, TN)
            value = lax.dot_general(
                hid[rows, cols], delta[rows, :], (((0,), (0,)), ((), ())), preferred_element_type=F32
            )
            grad[cols, :] = value if g == 0 else grad[cols, :] + value
            return carry

        lax.fori_loop(0, FF // TN, tile, 0)

    peers = (
        [(f, tpeer(k)) for k in range(1, NT)],
        [(fpeer(k) * 2 + c, t) for k in range(1, NF)],
        [(partner, t)],
    )

    def share(stage):
        return [
            rcopy(loss.at[stage], lrecv.at[7 * stage + i], ls_s.at[7 * stage + i], ls_r.at[7 * stage + i], pf, pt)
            for i, (pf, pt) in enumerate(peers[stage])
        ]

    def sum_up(stage):
        for cp in share(stage):
            cp.wait_recv()
        value = loss[stage]
        for i in range(len(peers[stage])):
            value = value + lrecv[7 * stage + i]
        loss[stage + 1] = value

    rcopy(tok_in, tok.at[rows_t(yo)], ty_s, ty_r, f, yo).wait_recv()
    for dz in range(1, 4):
        go(rcopy(tok.at[rows_t(yo)], tok.at[rows_t(yo)], tz_s.at[1, dz - 1], tz_r.at[1, dz - 1], f, tpeer(dz)))
    own_tok.wait()
    compact(0)
    for cp in local:
        cp.wait()
    rcopy(gw.at[:, other_cols], wts.at[his_c, pl.ds(0, HF)], w_s.at[0], w_r.at[0], partner, t).wait_recv()
    rcopy(uw.at[:, other_cols], wts.at[his_c, pl.ds(HF, HF)], w_s.at[1], w_r.at[1], partner, t).wait_recv()
    from_partner(0)
    gate_up(0)
    scatter_hidden(0)
    compact(1)
    from_partner(1)
    gate_up(1)
    scatter_hidden(1)
    gate_up(2)
    gate_up(3)
    reduce_hidden(0)
    scatter_hidden(2)
    reduce_hidden(1)
    scatter_hidden(3)
    down(0)
    reduce_hidden(2)
    down(1)
    reduce_hidden(3)
    make_delta(0)
    make_delta(1)
    down(2)
    make_delta(2)
    add_grad(0)
    down(3)
    add_grad(1)
    make_delta(3)
    for cp in share(0):
        go(cp)
    add_grad(2)
    sum_up(0)
    for cp in share(1):
        go(cp)
    add_grad(3)
    grad_copy = pltpu.make_async_copy(grad, grad_out, out_sem)
    grad_copy.start()
    sum_up(1)
    for cp in share(2):
        go(cp)
    sum_up(2)
    loss_out[...] = loss[3]
    for cp in sends:
        cp.wait_send()
    grad_copy.wait()


def shards(tokens, gate_weight, up_weight, down_frozen, down_learn, steer, sample_lengths):
    any_spec = pl.BlockSpec(memory_space=pl.ANY)
    vmem = pltpu.VMEM
    dma = pltpu.SemaphoreType.DMA
    rows = 2 * HALF
    grad_down, sums = pl.pallas_call(
        kernel,
        out_shape=(
            jax.ShapeDtypeStruct((FF, W), F32),
            jax.ShapeDtypeStruct((2, 8, 128), F32),
        ),
        in_specs=[
            pl.BlockSpec(memory_space=pltpu.SMEM),
            pl.BlockSpec(memory_space=pltpu.VMEM),
        ] + [any_spec] * 5,
        out_specs=(any_spec, pl.BlockSpec(memory_space=pltpu.VMEM)),
        scratch_shapes=[
            vmem((2 * RAW, W), BF16),
            vmem((rows, 2 * W), BF16),
            vmem((2 * W, FF), BF16),
            vmem((rows, FF), BF16),
            vmem((4, NF - 1, 48, FF), BF16),
            vmem((rows, FF), BF16),
            vmem((FF, W), BF16),
            vmem((FF, W), BF16),
            vmem((PART0, W), F32),
            vmem((rows, W), BF16),
            vmem((4, NT - 1, 48, W), BF16),
            vmem((rows, W), BF16),
            vmem((FF, W), F32),
            vmem((4, 2, 8, 128), F32),
            vmem((15, 2, 8, 128), F32),
            dma((2, 3)), dma((2, 3)), dma, dma, dma((5,)),
            dma((2,)), dma((2,)), dma((2,)), dma((2,)),
            dma((4, 7)), dma((4, 7)), dma((4, 7)), dma((4, 7)), dma((4,)), dma((4,)),
            dma((4, 7)), dma((4, 7)), dma((4, 7)), dma((4, 7)), dma((15,)), dma((15,)),
            dma,
        ],
        compiler_params=pltpu.CompilerParams(
            collective_id=0, has_side_effects=True, vmem_limit_bytes=60 * 1024 * 1024
        ),
    )(sample_lengths, steer.reshape(64, 128), tokens, gate_weight, up_weight, down_frozen, down_learn)
    counts = jnp.sum(sample_lengths, axis=1).astype(F32)
    losses = sums[:, 0, 0] / (counts * D)
    return (grad_down, losses)


def solution(mesh):
    return jax.shard_map(
        shards,
        mesh=mesh,
        in_specs=(
            P("tensor", "fsdp"),
            P("fsdp", "tensor"),
            P("fsdp", "tensor"),
            P("tensor", "fsdp"),
            P("tensor", "fsdp"),
            P(),
            P(),
        ),
        out_specs=(P("tensor", "fsdp"), P()),
        check_vma=False,
    )
```

time: 188 us -> 164 us (0.87)
  Pallas kernels: 177 us -> 158 us
  matrix products: 7.12 us -> 0 us
  local copies, waits for them, and re-layouts: 2.18 us -> 5.05 us
    pallas_call x1, Pallas kernels: 177 us -> 158 us  [shards(): pl.pallas_call(kernel, out_shape=(jax.ShapeDtypeStruct((FF, W), F32), jax...]
    dot_general x1 -> x0, matrix products: 7.12 us -> none  [shards(): lax.dot_general(hid, delta, (((0,), (0,)), ((), ())), preferred_element_t...]
    unnamed x2 -> x3, local copies, waits for them, and re-layouts: 0.01 us -> 4.25 us
where the time goes in v2:
time: 164 us
  Pallas kernels  158 us (96%)
  local copies, waits for them, and re-layouts  5.05 us (3%)
    pallas_call x1, Pallas kernels, shards(): pl.pallas_call(kernel, out_shape=(jax.ShapeDtypeStruct((FF, W), F32), jax...  158 us
    unnamed x3, local copies, waits for them, and re-layouts  4.25 us

profile of v2, /device:TPU:1, one launch (start us, length us, event | category | flops | bytes accessed | tf_op | source)
XLA Modules:
  0.0 163.9 jit_solution(10521784331068049401)
XLA Ops:
  0.6 0.0 copy-start
  0.6 157.5 %shard_map.86 = (f32[1792,512]{1,0:T(8,128)}, f32[2,8,128]{2,1,0:T(8,128)}) custom-call(s32[2,8]{1,0:T(2,128)} %lens.1, f32[64,128]{1,0:T(8,128)} %bitcast.1, bf16[256,512]{1,0:T(8,128)(2,1)} %tok_in.1, bf16[512,1792]{1,0:T(8,128)(2,1)} %gw.1, bf16[512,1792]{1,0:T(8,128)(2,1)} %uw.1, bf16[1792,512]{1,0:T(8,128)(2,1)} %wf_in.1, bf16[1792,512]{1,0:T(8,128)(2,1)} %wl_in.1), custom_call_target="tpu_custom_call" | custom-call | tf_op jit(solution)/shard_map/pallas_call | solution.py:348
  158.2 0.8 slice_reduce_fusion
  159.0 0.0 copy-done
  159.0 0.1 reduce_sum.9
  159.1 0.5 multiply_divide_fusion
  159.6 4.2 %copy.10 = f32[1792,512]{1,0:T(8,128)} copy(f32[1792,512]{1,0:T(8,128)} %get-tuple-element.8) | data formatting | bytes 7340032
Async XLA Ops:
  0.6 158.4 %copy-start = (s32[2,8]{1,0:T(2,128)S(1)}, s32[2,8]{1,0:T(2,128)}, u32[]{:S(2)}) copy-start(s32[2,8]{1,0:T(2,128)} %lens.1) | copy-start | bytes 196

commit v3 on v2

--- a/solution.py
+++ b/solution.py
@@ -38,7 +38,7 @@
 def kernel(
     lens, steer, tok_in, gw, uw, wf_in, wl_in,
     grad_out, loss_out,
-    tok, ctok, wts, send, recv, hid, wf, wl, acc, dsend, drecv, delta, grad, loss, lrecv,
+    tok, ctok, wts, send, recv, ysend, yrecv, own, hid, wf, wl, acc, dsend, drecv, delta, grad, loss, lrecv,
     tz_s, tz_r, ty_s, ty_r, loc, w_s, w_r, c_s, c_r, rs_s, rs_r, ag_s, ag_r, pr_s, pr_r,
     ds_s, ds_r, dg_s, dg_r, ls_s, ls_r, out_sem,
 ):
@@ -51,6 +51,7 @@
     yh = t // 4
     z = t % 4
     partner = f + 1 - 2 * c
+    yfold = f + 2 - 4 * yl
 
     def fpeer(k, sign=1):
         dx, dy = k // 2, k % 2
@@ -148,39 +149,77 @@
 
         lax.fori_loop(0, FF // TN, tile, 0)
 
-    def rs_copy(p, k):
-        part, n = CHUNKS[p]
-        to = fpeer(k)
+    def xs_copy(p, dx):
+        part, n = CHUNKS[p]
+        to = (x + dx) % 4
         return rcopy(
-            send.at[rows_of(kinds[p], part, to * n, n)], recv.at[p, k - 1, pl.ds(0, n)],
-            rs_s.at[p, k - 1], rs_r.at[p, k - 1], to * 2 + c, t,
+            send.at[rows_of(kinds[p], part, to * 2 * n, 2 * n)], recv.at[p, dx - 1, pl.ds(0, 2 * n)],
+            rs_s.at[p, dx - 1], rs_r.at[p, dx - 1], to * 4 + yl * 2 + c, t,
         )
 
+    def ys_copy(p):
+        n = CHUNKS[p][1]
+        return rcopy(ysend.at[p, pl.ds(0, n)], yrecv.at[p, pl.ds(0, n)], rs_s.at[p, 3], rs_r.at[p, 3], yfold, t)
+
     def scatter_hidden(p):
-        for k in range(1, NF):
-            go(rs_copy(p, k))
+        for dx in range(1, 4):
+            go(xs_copy(p, dx))
+
+    def reduce_x(p):
+        for dx in range(1, 4):
+            xs_copy(p, dx).wait_recv()
+        part, n = CHUNKS[p]
+
+        def total(j, half):
+            cols = at(j * 128, 128, 128)
+            value = decode(send[rows_of(kinds[p], part, (2 * x + half) * n, n), cols])
+            for k in range(3):
+                value += decode(recv[p, k, at(half * n, n), cols])
+            return value
+
+        def theirs(j, carry):
+            ysend[p, pl.ds(0, n), at(j * 128, 128, 128)] = encode(total(j, 1 - yl))
+            return carry
+
+        def ours(j, carry):
+            own[p, pl.ds(0, n), at(j * 128, 128, 128)] = total(j, yl)
+            return carry
+
+        lax.fori_loop(0, FF // 128, theirs, 0)
+        go(ys_copy(p))
+        lax.fori_loop(0, FF // 128, ours, 0)
+
+    def hidden_copy(p, row, i, to):
+        part, n = CHUNKS[p]
+        region = hid.at[rows_of(kinds[p], part, row * n, n), my_cols]
+        return rcopy(region, region, ag_s.at[p, i], ag_r.at[p, i], to, t)
+
+    def xpeer(dx):
+        return (x + dx) % 4 * 4 + yl * 2 + c
 
     def reduce_hidden(p):
-        for k in range(1, NF):
-            rs_copy(p, k).wait_recv()
+        ys_copy(p).wait_recv()
         part, n = CHUNKS[p]
         mine = rows_of(kinds[p], part, q * n, n)
 
         def tile(j, carry):
             gc = at(j * 128, 128, 128)
             uc = at(HF + j * 128, 128, 128)
-            gate = decode(send[mine, gc])
-            up = decode(send[mine, uc])
-            for k in range(NF - 1):
-                gate += decode(recv[p, k, pl.ds(0, n), gc])
-                up += decode(recv[p, k, pl.ds(0, n), uc])
+            gate = own[p, pl.ds(0, n), gc] + decode(yrecv[p, pl.ds(0, n), gc])
+            up = own[p, pl.ds(0, n), uc] + decode(yrecv[p, pl.ds(0, n), uc])
             hid[mine, at(c * HF + j * 128, 128, 128)] = (gate * jax.nn.sigmoid(gate) * up).astype(BF16)
             return carry
 
         lax.fori_loop(0, HF // 128, tile, 0)
-        for k in range(1, NF):
-            region = hid.at[mine, my_cols]
-            go(rcopy(region, region, ag_s.at[p, k - 1], ag_r.at[p, k - 1], fpeer(k) * 2 + c, t))
+        go(hidden_copy(p, q, 6, yfold))
+        for dx in range(1, 4):
+            go(hidden_copy(p, q, dx - 1, xpeer(dx)))
+
+    def forward_hidden(p):
+        other = 2 * x + 1 - yl
+        hidden_copy(p, other, 6, yfold).wait_recv()
+        for dx in range(1, 4):
+            go(hidden_copy(p, other, 2 + dx, xpeer(dx)))
 
     def ds_copy(g, kind, part, n, k):
         to = tpeer(k)
@@ -192,9 +231,10 @@
     def down(p):
         part, n = CHUNKS[p]
         kind, g = kinds[p], ids[p]
-        for k in range(1, NF):
-            region = hid.at[rows_of(kind, part, fpeer(k, -1) * n, n), my_cols]
-            rcopy(region, region, ag_s.at[p, k - 1], ag_r.at[p, k - 1], fpeer(k) * 2 + c, t).wait_recv()
+        for dx in range(1, 4):
+            source = (x + 4 - dx) % 4 * 2
+            hidden_copy(p, source + yl, dx - 1, xpeer(dx)).wait_recv()
+            hidden_copy(p, source + 1 - yl, 2 + dx, xpeer(dx)).wait_recv()
         rows = rows_of(kind, part, 0, NF * n)
         go(rcopy(hid.at[rows, my_cols], hid.at[rows, my_cols], pr_s.at[p], pr_r.at[p], partner, t))
 
@@ -305,14 +345,22 @@
     scatter_hidden(1)
     gate_up(2)
     gate_up(3)
+    reduce_x(0)
     reduce_hidden(0)
+    forward_hidden(0)
     scatter_hidden(2)
+    reduce_x(1)
     reduce_hidden(1)
+    forward_hidden(1)
     scatter_hidden(3)
     down(0)
+    reduce_x(2)
     reduce_hidden(2)
+    forward_hidden(2)
     down(1)
+    reduce_x(3)
     reduce_hidden(3)
+    forward_hidden(3)
     make_delta(0)
     make_delta(1)
     down(2)
@@ -361,7 +409,10 @@
             vmem((rows, 2 * W), BF16),
             vmem((2 * W, FF), BF16),
             vmem((rows, FF), BF16),
-            vmem((4, NF - 1, 48, FF), BF16),
+            vmem((4, 3, 96, FF), BF16),
+            vmem((4, 48, FF), BF16),
+            vmem((4, 48, FF), BF16),
+            vmem((4, 48, FF), F32),
             vmem((rows, FF), BF16),
             vmem((FF, W), BF16),
             vmem((FF, W), BF16),
@@ -374,7 +425,7 @@
             vmem((15, 2, 8, 128), F32),
             dma((2, 3)), dma((2, 3)), dma, dma, dma((5,)),
             dma((2,)), dma((2,)), dma((2,)), dma((2,)),
-            dma((4, 7)), dma((4, 7)), dma((4, 7)), dma((4, 7)), dma((4,)), dma((4,)),
+            dma((4, 4)), dma((4, 4)), dma((4, 7)), dma((4, 7)), dma((4,)), dma((4,)),
             dma((4, 7)), dma((4, 7)), dma((4, 7)), dma((4, 7)), dma((15,)), dma((15,)),
             dma,
         ],

time: 164 us -> 151 us (0.921)
  Pallas kernels: 158 us -> 145 us
    pallas_call x1, Pallas kernels: 158 us -> 145 us  [shards(): pl.pallas_call(kernel, out_shape=(jax.ShapeDtypeStruct((FF, W), F32), jax...]
where the time goes in v3:
time: 151 us
  Pallas kernels  145 us (96%)
  local copies, waits for them, and re-layouts  5.05 us (3%)
    pallas_call x1, Pallas kernels, shards(): pl.pallas_call(kernel, out_shape=(jax.ShapeDtypeStruct((FF, W), F32), jax...  145 us
    unnamed x3, local copies, waits for them, and re-layouts  4.25 us

profile of v3, /device:TPU:1, one launch (start us, length us, event | category | flops | bytes accessed | tf_op | source)
XLA Modules:
  0.0 150.9 jit_solution(7139847282722070645)
XLA Ops:
  0.6 0.0 copy-start
  0.6 144.5 %shard_map.86 = (f32[1792,512]{1,0:T(8,128)}, f32[2,8,128]{2,1,0:T(8,128)}) custom-call(s32[2,8]{1,0:T(2,128)} %lens.1, f32[64,128]{1,0:T(8,128)} %bitcast.1, bf16[256,512]{1,0:T(8,128)(2,1)} %tok_in.1, bf16[512,1792]{1,0:T(8,128)(2,1)} %gw.1, bf16[512,1792]{1,0:T(8,128)(2,1)} %uw.1, bf16[1792,512]{1,0:T(8,128)(2,1)} %wf_in.1, bf16[1792,512]{1,0:T(8,128)(2,1)} %wl_in.1), custom_call_target="tpu_custom_call" | custom-call | tf_op jit(solution)/shard_map/pallas_call | solution.py:396
  145.2 0.8 slice_reduce_fusion
  146.0 0.0 copy-done
  146.0 0.1 reduce_sum.9
  146.1 0.5 multiply_divide_fusion
  146.6 4.2 %copy.10 = f32[1792,512]{1,0:T(8,128)} copy(f32[1792,512]{1,0:T(8,128)} %get-tuple-element.8) | data formatting | bytes 7340032
Async XLA Ops:
  0.6 145.4 %copy-start = (s32[2,8]{1,0:T(2,128)S(1)}, s32[2,8]{1,0:T(2,128)}, u32[]{:S(2)}) copy-start(s32[2,8]{1,0:T(2,128)} %lens.1) | copy-start | bytes 196

commit v4 on v3

--- a/solution.py
+++ b/solution.py
@@ -38,7 +38,7 @@
 def kernel(
     lens, steer, tok_in, gw, uw, wf_in, wl_in,
     grad_out, loss_out,
-    tok, ctok, wts, send, recv, ysend, yrecv, own, hid, wf, wl, acc, dsend, drecv, delta, grad, loss, lrecv,
+    tok, ctok, picks, wts, send, gx_in, gy_out, gy_in, uy_in, ux_out, ux_in, own, hid, wf, wl, acc, dsend, drecv, delta, grad, loss, lrecv,
     tz_s, tz_r, ty_s, ty_r, loc, w_s, w_r, c_s, c_r, rs_s, rs_r, ag_s, ag_r, pr_s, pr_r,
     ds_s, ds_r, dg_s, dg_r, ls_s, ls_r, out_sem,
 ):
@@ -57,6 +57,9 @@
         dx, dy = k // 2, k % 2
         return ((x + 4 + sign * dx) % 4) * 2 + (yl + dy) % 2
 
+    def xpeer(dx):
+        return (x + dx) % 4 * 4 + yl * 2 + c
+
     def tpeer(k, sign=1):
         dy, dz = k // 4, k % 4
         return ((yh + dy) % 2) * 4 + (z + 4 + sign * dz) % 4
@@ -90,9 +93,10 @@
     barrier = pltpu.get_barrier_semaphore()
     for k in range(1, NF):
         pl.semaphore_signal(barrier, inc=1, device_id=(fpeer(k) * 2 + c, t), device_id_type=MESH)
+        pl.semaphore_signal(barrier, inc=1, device_id=(fpeer(k) * 2 + 1 - c, t), device_id_type=MESH)
         pl.semaphore_signal(barrier, inc=1, device_id=(f, tpeer(k)), device_id_type=MESH)
     pl.semaphore_signal(barrier, inc=1, device_id=(partner, t), device_id_type=MESH)
-    pl.semaphore_wait(barrier, 15)
+    pl.semaphore_wait(barrier, 22)
 
     sends = []
     outs = []
@@ -115,22 +119,23 @@
     def rows_of(kind, part, start, size):
         return at(base_of(kind, part) + start, size)
 
+    def pick(i):
+        rid = lax.broadcasted_iota(jnp.int32, (HALF, SLOT), 0)
+        lane = lax.broadcasted_iota(jnp.int32, (HALF, SLOT), 1)
+        off = jnp.int32(0)
+        for k in range(SEQS):
+            n = jnp.where(kinds[i] == 0, lens[0, k], lens[1, k])
+            picks[i, :, pl.ds(k * SLOT, SLOT)] = jnp.where((rid == off + lane) & (lane < n), 1.0, 0.0).astype(BF16)
+            off = off + n
+
     def compact(i):
         kind = kinds[i]
         for dz in range(1, 4):
             s = tpeer(dz + 4 * i, -1)
             rcopy(tok_in, tok.at[rows_t(s)], tz_s.at[i, dz - 1], tz_r.at[i, dz - 1], f, s).wait_recv()
-        rid = lax.broadcasted_iota(jnp.int32, (HALF, SLOT), 0)
-        lane = lax.broadcasted_iota(jnp.int32, (HALF, SLOT), 1)
-        off = jnp.int32(0)
-        picks = []
-        for k in range(SEQS):
-            n = jnp.where(kind == 0, lens[0, k], lens[1, k])
-            picks.append(jnp.where((rid == off + lane) & (lane < n), 1.0, 0.0).astype(BF16))
-            off = off + n
         hr = at(kind * HALF, HALF)
         ctok[hr, mine_c] = jnp.dot(
-            jnp.concatenate(picks, axis=1), tok[at(kind * RAW, RAW), :], preferred_element_type=F32
+            picks[i], tok[at(kind * RAW, RAW), :], preferred_element_type=F32
         ).astype(BF16)
         go(rcopy(ctok.at[hr, mine_c], ctok.at[hr, mine_c], c_s.at[i], c_r.at[i], partner, t))
 
@@ -149,64 +154,98 @@
 
         lax.fori_loop(0, FF // TN, tile, 0)
 
-    def xs_copy(p, dx):
+    def gx_copy(p, dx):
         part, n = CHUNKS[p]
         to = (x + dx) % 4
         return rcopy(
-            send.at[rows_of(kinds[p], part, to * 2 * n, 2 * n)], recv.at[p, dx - 1, pl.ds(0, 2 * n)],
-            rs_s.at[p, dx - 1], rs_r.at[p, dx - 1], to * 4 + yl * 2 + c, t,
+            send.at[rows_of(kinds[p], part, to * 2 * n, 2 * n), pl.ds(0, HF)], gx_in.at[p, dx - 1, pl.ds(0, 2 * n)],
+            rs_s.at[p, dx - 1], rs_r.at[p, dx - 1], xpeer(dx), t,
         )
 
-    def ys_copy(p):
+    def gy_copy(p):
         n = CHUNKS[p][1]
-        return rcopy(ysend.at[p, pl.ds(0, n)], yrecv.at[p, pl.ds(0, n)], rs_s.at[p, 3], rs_r.at[p, 3], yfold, t)
+        return rcopy(gy_out.at[p, pl.ds(0, n)], gy_in.at[p, pl.ds(0, n)], rs_s.at[p, 3], rs_r.at[p, 3], yfold, t)
+
+    def uy_copy(p, i):
+        part, n = CHUNKS[p]
+        return rcopy(
+            send.at[rows_of(kinds[p], part, (2 * i + 1 - yl) * n, n), pl.ds(HF, HF)], uy_in.at[p, i, pl.ds(0, n)],
+            rs_s.at[p, 4 + i], rs_r.at[p, 4 + i], yfold, t,
+        )
+
+    def ux_copy(p, dx):
+        n = CHUNKS[p][1]
+        return rcopy(
+            ux_out.at[p, dx, pl.ds(0, n)], ux_in.at[p, dx - 1, pl.ds(0, n)],
+            rs_s.at[p, 7 + dx], rs_r.at[p, 7 + dx], xpeer(dx), t,
+        )
 
     def scatter_hidden(p):
         for dx in range(1, 4):
-            go(xs_copy(p, dx))
+            go(gx_copy(p, dx))
+        for i in range(4):
+            go(uy_copy(p, i))
 
     def reduce_x(p):
-        for dx in range(1, 4):
-            xs_copy(p, dx).wait_recv()
-        part, n = CHUNKS[p]
-
-        def total(j, half):
+        part, n = CHUNKS[p]
+
+        def gate_sum(j, half):
             cols = at(j * 128, 128, 128)
             value = decode(send[rows_of(kinds[p], part, (2 * x + half) * n, n), cols])
             for k in range(3):
-                value += decode(recv[p, k, at(half * n, n), cols])
+                value += decode(gx_in[p, k, at(half * n, n), cols])
             return value
 
-        def theirs(j, carry):
-            ysend[p, pl.ds(0, n), at(j * 128, 128, 128)] = encode(total(j, 1 - yl))
-            return carry
-
-        def ours(j, carry):
-            own[p, pl.ds(0, n), at(j * 128, 128, 128)] = total(j, yl)
-            return carry
-
-        lax.fori_loop(0, FF // 128, theirs, 0)
-        go(ys_copy(p))
-        lax.fori_loop(0, FF // 128, ours, 0)
+        def up_sum(j, i):
+            cols = at(j * 128, 128, 128)
+            value = decode(send[rows_of(kinds[p], part, (2 * i + yl) * n, n), at(HF + j * 128, 128, 128)])
+            return value + decode(uy_in[p, i, pl.ds(0, n), cols])
+
+        def gate_out(j, carry):
+            gy_out[p, pl.ds(0, n), at(j * 128, 128, 128)] = encode(gate_sum(j, 1 - yl))
+            return carry
+
+        def up_out(j, carry):
+            for dx in range(1, 4):
+                ux_out[p, dx, pl.ds(0, n), at(j * 128, 128, 128)] = encode(up_sum(j, (x + dx) % 4))
+            return carry
+
+        def keep(j, carry):
+            cols = at(j * 128, 128, 128)
+            own[p, pl.ds(0, n), cols] = gate_sum(j, yl)
+            own[p, pl.ds(0, n), at(HF + j * 128, 128, 128)] = up_sum(j, x)
+            return carry
+
+        for i in range(4):
+            uy_copy(p, i).wait_recv()
+        lax.fori_loop(0, HF // 128, up_out, 0)
+        for dx in range(1, 4):
+            go(ux_copy(p, dx))
+        for dx in range(1, 4):
+            gx_copy(p, dx).wait_recv()
+        lax.fori_loop(0, HF // 128, gate_out, 0)
+        go(gy_copy(p))
+        lax.fori_loop(0, HF // 128, keep, 0)
 
     def hidden_copy(p, row, i, to):
         part, n = CHUNKS[p]
         region = hid.at[rows_of(kinds[p], part, row * n, n), my_cols]
         return rcopy(region, region, ag_s.at[p, i], ag_r.at[p, i], to, t)
 
-    def xpeer(dx):
-        return (x + dx) % 4 * 4 + yl * 2 + c
-
     def reduce_hidden(p):
-        ys_copy(p).wait_recv()
+        gy_copy(p).wait_recv()
+        for dx in range(1, 4):
+            ux_copy(p, dx).wait_recv()
         part, n = CHUNKS[p]
         mine = rows_of(kinds[p], part, q * n, n)
 
         def tile(j, carry):
             gc = at(j * 128, 128, 128)
             uc = at(HF + j * 128, 128, 128)
-            gate = own[p, pl.ds(0, n), gc] + decode(yrecv[p, pl.ds(0, n), gc])
-            up = own[p, pl.ds(0, n), uc] + decode(yrecv[p, pl.ds(0, n), uc])
+            gate = own[p, pl.ds(0, n), gc] + decode(gy_in[p, pl.ds(0, n), gc])
+            up = own[p, pl.ds(0, n), uc]
+            for k in range(3):
+                up += decode(ux_in[p, k, pl.ds(0, n), gc])
             hid[mine, at(c * HF + j * 128, 128, 128)] = (gate * jax.nn.sigmoid(gate) * up).astype(BF16)
             return carry
 
@@ -303,14 +342,19 @@
                 hid[rows, cols], delta[rows, :], (((0,), (0,)), ((), ())), preferred_element_type=F32
             )
             grad[cols, :] = value if g == 0 else grad[cols, :] + value
+            if g == 3:
+                pltpu.make_async_copy(grad.at[cols], grad_out.at[cols], out_sem.at[j]).start()
             return carry
 
         lax.fori_loop(0, FF // TN, tile, 0)
+        if g == 3:
+            for j in range(FF // TN):
+                cols = pl.ds(j * TN, TN)
+                outs.append(pltpu.make_async_copy(grad.at[cols], grad_out.at[cols], out_sem.at[j]))
 
     peers = (
         [(f, tpeer(k)) for k in range(1, NT)],
-        [(fpeer(k) * 2 + c, t) for k in range(1, NF)],
-        [(partner, t)],
+        [(fpeer(k) * 2 + (c if i == 0 else 1 - c), t) for k in range(NF) for i in range(2) if k or i],
     )
 
     def share(stage):
@@ -327,6 +371,8 @@
             value = value + lrecv[7 * stage + i]
         loss[stage + 1] = value
 
+    pick(0)
+    pick(1)
     rcopy(tok_in, tok.at[rows_t(yo)], ty_s, ty_r, f, yo).wait_recv()
     for dz in range(1, 4):
         go(rcopy(tok.at[rows_t(yo)], tok.at[rows_t(yo)], tz_s.at[1, dz - 1], tz_r.at[1, dz - 1], f, tpeer(dz)))
@@ -343,30 +389,30 @@
     from_partner(1)
     gate_up(1)
     scatter_hidden(1)
+    reduce_x(0)
     gate_up(2)
+    scatter_hidden(2)
     gate_up(3)
-    reduce_x(0)
+    reduce_x(1)
     reduce_hidden(0)
     forward_hidden(0)
-    scatter_hidden(2)
-    reduce_x(1)
+    scatter_hidden(3)
+    reduce_x(2)
     reduce_hidden(1)
     forward_hidden(1)
-    scatter_hidden(3)
     down(0)
-    reduce_x(2)
+    reduce_x(3)
     reduce_hidden(2)
     forward_hidden(2)
     down(1)
-    reduce_x(3)
     reduce_hidden(3)
     forward_hidden(3)
     make_delta(0)
     make_delta(1)
     down(2)
+    down(3)
+    add_grad(0)
     make_delta(2)
-    add_grad(0)
-    down(3)
     add_grad(1)
     make_delta(3)
     for cp in share(0):
@@ -376,16 +422,16 @@
     for cp in share(1):
         go(cp)
     add_grad(3)
-    grad_copy = pltpu.make_async_copy(grad, grad_out, out_sem)
-    grad_copy.start()
     sum_up(1)
-    for cp in share(2):
-        go(cp)
-    sum_up(2)
-    loss_out[...] = loss[3]
+    for kind in range(2):
+        count = jnp.float32(0)
+        for k in range(SEQS):
+            count = count + lens[kind, k].astype(F32)
+        loss_out[kind] = jnp.max(loss[2, kind]) / (count * D)
     for cp in sends:
         cp.wait_send()
-    grad_copy.wait()
+    for cp in outs:
+        cp.wait()
 
 
 def shards(tokens, gate_weight, up_weight, down_frozen, down_learn, steer, sample_lengths):
@@ -393,25 +439,29 @@
     vmem = pltpu.VMEM
     dma = pltpu.SemaphoreType.DMA
     rows = 2 * HALF
-    grad_down, sums = pl.pallas_call(
+    return pl.pallas_call(
         kernel,
         out_shape=(
             jax.ShapeDtypeStruct((FF, W), F32),
-            jax.ShapeDtypeStruct((2, 8, 128), F32),
+            jax.ShapeDtypeStruct((2,), F32),
         ),
         in_specs=[
             pl.BlockSpec(memory_space=pltpu.SMEM),
             pl.BlockSpec(memory_space=pltpu.VMEM),
         ] + [any_spec] * 5,
-        out_specs=(any_spec, pl.BlockSpec(memory_space=pltpu.VMEM)),
+        out_specs=(any_spec, pl.BlockSpec(memory_space=pltpu.SMEM)),
         scratch_shapes=[
             vmem((2 * RAW, W), BF16),
             vmem((rows, 2 * W), BF16),
+            vmem((2, HALF, RAW), BF16),
             vmem((2 * W, FF), BF16),
             vmem((rows, FF), BF16),
-            vmem((4, 3, 96, FF), BF16),
-            vmem((4, 48, FF), BF16),
-            vmem((4, 48, FF), BF16),
+            vmem((4, 3, 96, HF), BF16),
+            vmem((4, 48, HF), BF16),
+            vmem((4, 48, HF), BF16),
+            vmem((4, 4, 48, HF), BF16),
+            vmem((4, 4, 48, HF), BF16),
+            vmem((4, 3, 48, HF), BF16),
             vmem((4, 48, FF), F32),
             vmem((rows, FF), BF16),
             vmem((FF, W), BF16),
@@ -421,21 +471,18 @@
             vmem((4, NT - 1, 48, W), BF16),
             vmem((rows, W), BF16),
             vmem((FF, W), F32),
-            vmem((4, 2, 8, 128), F32),
-            vmem((15, 2, 8, 128), F32),
+            vmem((3, 2, 8, 128), F32),
+            vmem((22, 2, 8, 128), F32),
             dma((2, 3)), dma((2, 3)), dma, dma, dma((5,)),
             dma((2,)), dma((2,)), dma((2,)), dma((2,)),
-            dma((4, 4)), dma((4, 4)), dma((4, 7)), dma((4, 7)), dma((4,)), dma((4,)),
-            dma((4, 7)), dma((4, 7)), dma((4, 7)), dma((4, 7)), dma((15,)), dma((15,)),
-            dma,
+            dma((4, 11)), dma((4, 11)), dma((4, 7)), dma((4, 7)), dma((4,)), dma((4,)),
+            dma((4, 7)), dma((4, 7)), dma((4, 7)), dma((4, 7)), dma((22,)), dma((22,)),
+            dma((7,)),
         ],
         compiler_params=pltpu.CompilerParams(
             collective_id=0, has_side_effects=True, vmem_limit_bytes=60 * 1024 * 1024
         ),
     )(sample_lengths, steer.reshape(64, 128), tokens, gate_weight, up_weight, down_frozen, down_learn)
-    counts = jnp.sum(sample_lengths, axis=1).astype(F32)
-    losses = sums[:, 0, 0] / (counts * D)
-    return (grad_down, losses)
 
 
 def solution(mesh):

time: 151 us -> 134 us (0.89)
  Pallas kernels: 145 us -> 129 us
    pallas_call x1, Pallas kernels: 145 us -> 129 us  [shards(): pl.pallas_call(kernel, out_shape=(jax.ShapeDtypeStruct((FF, W), F32), jax...]
    unnamed x3 -> x4, local copies, waits for them, and re-layouts: 4.25 us -> 4.76 us
where the time goes in v4:
time: 134 us
  Pallas kernels  129 us (96%)
  local copies, waits for them, and re-layouts  4.76 us (4%)
    pallas_call x1, Pallas kernels, shards(): pl.pallas_call(kernel, out_shape=(jax.ShapeDtypeStruct((FF, W), F32), jax...  129 us
    unnamed x4, local copies, waits for them, and re-layouts  4.76 us

profile of v4, /device:TPU:1, one launch (start us, length us, event | category | flops | bytes accessed | tf_op | source)
XLA Modules:
  0.0 134.0 jit_solution(14743138665891189490)
XLA Ops:
  0.6 128.6 %shard_map.86 = (f32[1792,512]{1,0:T(8,128)}, f32[2]{0:T(128)}) custom-call(s32[2,8]{1,0:T(2,128)} %lens.1, f32[64,128]{1,0:T(8,128)} %bitcast.1, bf16[256,512]{1,0:T(8,128)(2,1)} %tok_in.1, bf16[512,1792]{1,0:T(8,128)(2,1)} %gw.1, bf16[512,1792]{1,0:T(8,128)(2,1)} %uw.1, bf16[1792,512]{1,0:T(8,128)(2,1)} %wf_in.1, bf16[1792,512]{1,0:T(8,128)(2,1)} %wl_in.1), custom_call_target="tpu_custom_call" | custom-call | tf_op jit(solution)/shard_map/pallas_call | solution.py:442
  129.3 0.0 copy-start
  129.3 4.2 %copy.11 = f32[1792,512]{1,0:T(8,128)} copy(f32[1792,512]{1,0:T(8,128)} %get-tuple-element.4) | data formatting | bytes 7340032
  133.5 0.0 copy-done
  133.5 0.5 copy.12
Async XLA Ops:
  129.3 4.3 %copy-start = (f32[2]{0:T(128)S(1)}, f32[2]{0:T(128)}, u32[]{:S(2)}) copy-start(f32[2]{0:T(128)} %get-tuple-element.5) | copy-start | bytes 28

commit v5 on v4

--- a/solution.py
+++ b/solution.py
@@ -33,6 +33,7 @@
 
 CHUNKS = ((0, 48), (0, 48), (1, 32), (1, 32))
 PART0 = 384
+X_FIRST = (True, False, False, False)
 
 
 def kernel(
@@ -255,10 +256,16 @@
             go(hidden_copy(p, q, dx - 1, xpeer(dx)))
 
     def forward_hidden(p):
-        other = 2 * x + 1 - yl
-        hidden_copy(p, other, 6, yfold).wait_recv()
-        for dx in range(1, 4):
-            go(hidden_copy(p, other, 2 + dx, xpeer(dx)))
+        if not X_FIRST[p]:
+            other = 2 * x + 1 - yl
+            hidden_copy(p, other, 6, yfold).wait_recv()
+            for dx in range(1, 4):
+                go(hidden_copy(p, other, 2 + dx, xpeer(dx)))
+            return
+        for dx in range(1, 4):
+            source = (x + 4 - dx) % 4 * 2 + yl
+            hidden_copy(p, source, dx - 1, xpeer(dx)).wait_recv()
+            go(hidden_copy(p, source, 2 + dx, yfold))
 
     def ds_copy(g, kind, part, n, k):
         to = tpeer(k)
@@ -267,15 +274,22 @@
             ds_s.at[g, k - 1], ds_r.at[g, k - 1], f, to,
         )
 
+    def relay(p):
+        part, n = CHUNKS[p]
+        if X_FIRST[p]:
+            hidden_copy(p, 2 * x + 1 - yl, 6, yfold).wait_recv()
+        for dx in range(1, 4):
+            source = (x + 4 - dx) % 4 * 2
+            if not X_FIRST[p]:
+                hidden_copy(p, source + yl, dx - 1, xpeer(dx)).wait_recv()
+            hidden_copy(p, source + 1 - yl, 2 + dx, xpeer(dx)).wait_recv()
+        rows = rows_of(kinds[p], part, 0, NF * n)
+        go(rcopy(hid.at[rows, my_cols], hid.at[rows, my_cols], pr_s.at[p], pr_r.at[p], partner, t))
+
     def down(p):
         part, n = CHUNKS[p]
         kind, g = kinds[p], ids[p]
-        for dx in range(1, 4):
-            source = (x + 4 - dx) % 4 * 2
-            hidden_copy(p, source + yl, dx - 1, xpeer(dx)).wait_recv()
-            hidden_copy(p, source + 1 - yl, 2 + dx, xpeer(dx)).wait_recv()
         rows = rows_of(kind, part, 0, NF * n)
-        go(rcopy(hid.at[rows, my_cols], hid.at[rows, my_cols], pr_s.at[p], pr_r.at[p], partner, t))
 
         def product(contract, cols):
             value = jnp.dot(hid[rows, contract], wl[contract, cols], preferred_element_type=F32)
@@ -324,6 +338,9 @@
             delta[mine, :] = (2.0 * value).astype(BF16)
         square = jnp.broadcast_to(jnp.sum(diff * diff, keepdims=True), (8, 128))
         loss[0, kind] = square if part == 0 else loss[0, kind] + square
+        if g == 3:
+            for cp in share(0):
+                go(cp)
         for k in range(1, NT):
             go(rcopy(delta.at[mine], delta.at[mine], dg_s.at[g, k - 1], dg_r.at[g, k - 1], f, tpeer(k)))
 
@@ -395,28 +412,30 @@
     gate_up(3)
     reduce_x(1)
     reduce_hidden(0)
-    forward_hidden(0)
     scatter_hidden(3)
     reduce_x(2)
     reduce_hidden(1)
+    forward_hidden(0)
     forward_hidden(1)
-    down(0)
     reduce_x(3)
     reduce_hidden(2)
+    relay(0)
+    down(0)
     forward_hidden(2)
+    relay(1)
     down(1)
     reduce_hidden(3)
     forward_hidden(3)
+    relay(2)
     make_delta(0)
     make_delta(1)
     down(2)
+    relay(3)
     down(3)
     add_grad(0)
     make_delta(2)
     add_grad(1)
     make_delta(3)
-    for cp in share(0):
-        go(cp)
     add_grad(2)
     sum_up(0)
     for cp in share(1):

time: 134 us -> 130 us (0.970)
  Pallas kernels: 129 us -> 124 us
    pallas_call x1, Pallas kernels: 129 us -> 124 us  [shards(): pl.pallas_call(kernel, out_shape=(jax.ShapeDtypeStruct((FF, W), F32), jax...]
where the time goes in v5:
time: 130 us
  Pallas kernels  124 us (95%)
  local copies, waits for them, and re-layouts  4.76 us (4%)
    pallas_call x1, Pallas kernels, shards(): pl.pallas_call(kernel, out_shape=(jax.ShapeDtypeStruct((FF, W), F32), jax...  124 us
    unnamed x4, local copies, waits for them, and re-layouts  4.76 us

profile of v5, /device:TPU:1, one launch (start us, length us, event | category | flops | bytes accessed | tf_op | source)
XLA Modules:
  0.0 129.8 jit_solution(1210613990832604962)
XLA Ops:
  0.6 124.4 %shard_map.86 = (f32[1792,512]{1,0:T(8,128)}, f32[2]{0:T(128)}) custom-call(s32[2,8]{1,0:T(2,128)} %lens.1, f32[64,128]{1,0:T(8,128)} %bitcast.1, bf16[256,512]{1,0:T(8,128)(2,1)} %tok_in.1, bf16[512,1792]{1,0:T(8,128)(2,1)} %gw.1, bf16[512,1792]{1,0:T(8,128)(2,1)} %uw.1, bf16[1792,512]{1,0:T(8,128)(2,1)} %wf_in.1, bf16[1792,512]{1,0:T(8,128)(2,1)} %wl_in.1), custom_call_target="tpu_custom_call" | custom-call | tf_op jit(solution)/shard_map/pallas_call | solution.py:461
  125.0 0.0 copy-start
  125.0 4.2 %copy.11 = f32[1792,512]{1,0:T(8,128)} copy(f32[1792,512]{1,0:T(8,128)} %get-tuple-element.4) | data formatting | bytes 7340032
  129.3 0.0 copy-done
  129.3 0.5 copy.12
Async XLA Ops:
  125.0 4.3 %copy-start = (f32[2]{0:T(128)S(1)}, f32[2]{0:T(128)}, u32[]{:S(2)}) copy-start(f32[2]{0:T(128)} %get-tuple-element.5) | copy-start | bytes 28

commit v6 on v5

--- a/solution.py
+++ b/solution.py
@@ -144,16 +144,20 @@
         hr = at(kinds[i] * HALF, HALF)
         rcopy(ctok.at[hr, mine_c], ctok.at[hr, his_c], c_s.at[i], c_r.at[i], partner, t).wait_recv()
 
-    def gate_up(p):
+    def gate_up(p, blocks=((0, 512), (512, 384), (HF, 512), (HF + 512, 384))):
         part, n = CHUNKS[p]
         rows = rows_of(kinds[p], part, 0, NF * n)
-
-        def tile(j, carry):
-            cols = at(j * TN, TN, TN)
+        for start, size in blocks:
+            cols = pl.ds(start, size)
             send[rows, cols] = encode(jnp.dot(ctok[rows, :], wts[:, cols], preferred_element_type=F32))
-            return carry
-
-        lax.fori_loop(0, FF // TN, tile, 0)
+
+    def gate_up_send(p):
+        gate_up(p, ((0, 512), (512, 384)))
+        for dx in range(1, 4):
+            go(gx_copy(p, dx))
+        gate_up(p, ((HF, 512), (HF + 512, 384)))
+        for i in range(4):
+            go(uy_copy(p, i))
 
     def gx_copy(p, dx):
         part, n = CHUNKS[p]
@@ -400,12 +404,10 @@
     rcopy(gw.at[:, other_cols], wts.at[his_c, pl.ds(0, HF)], w_s.at[0], w_r.at[0], partner, t).wait_recv()
     rcopy(uw.at[:, other_cols], wts.at[his_c, pl.ds(HF, HF)], w_s.at[1], w_r.at[1], partner, t).wait_recv()
     from_partner(0)
-    gate_up(0)
-    scatter_hidden(0)
+    gate_up_send(0)
     compact(1)
     from_partner(1)
-    gate_up(1)
-    scatter_hidden(1)
+    gate_up_send(1)
     reduce_x(0)
     gate_up(2)
     scatter_hidden(2)
@@ -438,16 +440,22 @@
     make_delta(3)
     add_grad(2)
     sum_up(0)
+    early = len(sends)
     for cp in share(1):
         go(cp)
     add_grad(3)
+    counts = []
+    for kind in range(2):
+        count = lens[kind, 0]
+        for k in range(1, SEQS):
+            count = count + lens[kind, k]
+        counts.append(count.astype(F32) * D)
+    for cp in sends[:early]:
+        cp.wait_send()
     sum_up(1)
     for kind in range(2):
-        count = jnp.float32(0)
-        for k in range(SEQS):
-            count = count + lens[kind, k].astype(F32)
-        loss_out[kind] = jnp.max(loss[2, kind]) / (count * D)
-    for cp in sends:
+        loss_out[kind] = loss[2, kind][0, 0] / counts[kind]
+    for cp in sends[early:]:
         cp.wait_send()
     for cp in outs:
         cp.wait()

time: 130 us -> 128 us (0.985)
  Pallas kernels: 124 us -> 122 us
    pallas_call x1, Pallas kernels: 124 us -> 122 us  [shards(): pl.pallas_call(kernel, out_shape=(jax.ShapeDtypeStruct((FF, W), F32), jax...]
where the time goes in v6:
time: 128 us
  Pallas kernels  122 us (95%)
  local copies, waits for them, and re-layouts  4.76 us (4%)
    pallas_call x1, Pallas kernels, shards(): pl.pallas_call(kernel, out_shape=(jax.ShapeDtypeStruct((FF, W), F32), jax...  122 us
    unnamed x4, local copies, waits for them, and re-layouts  4.76 us

profile of v6, /device:TPU:1, one launch (start us, length us, event | category | flops | bytes accessed | tf_op | source)
XLA Modules:
  0.0 127.8 jit_solution(7221814833772171283)
XLA Ops:
  0.6 122.4 %shard_map.86 = (f32[1792,512]{1,0:T(8,128)}, f32[2]{0:T(128)}) custom-call(s32[2,8]{1,0:T(2,128)} %lens.1, f32[64,128]{1,0:T(8,128)} %bitcast.1, bf16[256,512]{1,0:T(8,128)(2,1)} %tok_in.1, bf16[512,1792]{1,0:T(8,128)(2,1)} %gw.1, bf16[512,1792]{1,0:T(8,128)(2,1)} %uw.1, bf16[1792,512]{1,0:T(8,128)(2,1)} %wf_in.1, bf16[1792,512]{1,0:T(8,128)(2,1)} %wl_in.1), custom_call_target="tpu_custom_call" | custom-call | tf_op jit(solution)/shard_map/pallas_call | solution.py:469
  123.0 0.0 copy-start
  123.0 4.2 %copy.11 = f32[1792,512]{1,0:T(8,128)} copy(f32[1792,512]{1,0:T(8,128)} %get-tuple-element.4) | data formatting | bytes 7340032
  127.3 0.0 copy-done
  127.3 0.5 copy.12
Async XLA Ops:
  123.0 4.3 %copy-start = (f32[2]{0:T(128)S(1)}, f32[2]{0:T(128)}, u32[]{:S(2)}) copy-start(f32[2]{0:T(128)} %get-tuple-element.5) | copy-start | bytes 28

commit v7 on v6

--- a/solution.py
+++ b/solution.py
@@ -345,13 +345,28 @@
         if g == 3:
             for cp in share(0):
                 go(cp)
-        for k in range(1, NT):
+        for k in range(1, NT if g > 1 else 5):
             go(rcopy(delta.at[mine], delta.at[mine], dg_s.at[g, k - 1], dg_r.at[g, k - 1], f, tpeer(k)))
+
+    def delta_copy(g, source, i, to):
+        part, n = CHUNKS[g]
+        region = delta.at[rows_of(g % 2, part, source * n, n)]
+        return rcopy(region, region, dg_s.at[g, i], dg_r.at[g, i], f, to)
+
+    def pass_delta(g):
+        if g == 1:
+            delta_copy(g, yo, 3, yo).wait_recv()
+        for k in range(1, 4):
+            if g == 0:
+                delta_copy(g, tpeer(k, -1), k - 1, tpeer(k)).wait_recv()
+                go(delta_copy(g, tpeer(k, -1), 3 + k, yo))
+            else:
+                go(delta_copy(g, yo, 3 + k, tpeer(k)))
 
     def add_grad(g):
         kind = g % 2
         part, n = CHUNKS[g]
-        for k in range(1, NT):
+        for k in ((4, 5, 6, 7), (1, 2, 3, 5, 6, 7), range(1, NT), range(1, NT))[g]:
             who = tpeer(k, -1)
             region = delta.at[rows_of(kind, part, who * n, n)]
             rcopy(region, region, dg_s.at[g, k - 1], dg_r.at[g, k - 1], f, who).wait_recv()
@@ -434,10 +449,12 @@
     down(2)
     relay(3)
     down(3)
+    pass_delta(0)
+    pass_delta(1)
+    make_delta(2)
     add_grad(0)
-    make_delta(2)
+    make_delta(3)
     add_grad(1)
-    make_delta(3)
     add_grad(2)
     sum_up(0)
     early = len(sends)

time: 128 us -> 127 us (level)
  no operation moved by 1% of the time
where the time goes in v7:
time: 127 us
  Pallas kernels  121 us (95%)
  local copies, waits for them, and re-layouts  4.76 us (4%)
    pallas_call x1, Pallas kernels, shards(): pl.pallas_call(kernel, out_shape=(jax.ShapeDtypeStruct((FF, W), F32), jax...  121 us
    unnamed x4, local copies, waits for them, and re-layouts  4.76 us

profile of v7, /device:TPU:1, one launch (start us, length us, event | category | flops | bytes accessed | tf_op | source)
XLA Modules:
  0.0 126.9 jit_solution(1061745021445154577)
XLA Ops:
  0.6 121.4 %shard_map.86 = (f32[1792,512]{1,0:T(8,128)}, f32[2]{0:T(128)}) custom-call(s32[2,8]{1,0:T(2,128)} %lens.1, f32[64,128]{1,0:T(8,128)} %bitcast.1, bf16[256,512]{1,0:T(8,128)(2,1)} %tok_in.1, bf16[512,1792]{1,0:T(8,128)(2,1)} %gw.1, bf16[512,1792]{1,0:T(8,128)(2,1)} %uw.1, bf16[1792,512]{1,0:T(8,128)(2,1)} %wf_in.1, bf16[1792,512]{1,0:T(8,128)(2,1)} %wl_in.1), custom_call_target="tpu_custom_call" | custom-call | tf_op jit(solution)/shard_map/pallas_call | solution.py:486
  122.1 0.0 copy-start
  122.1 4.2 %copy.11 = f32[1792,512]{1,0:T(8,128)} copy(f32[1792,512]{1,0:T(8,128)} %get-tuple-element.4) | data formatting | bytes 7340032
  126.3 0.0 copy-done
  126.3 0.5 copy.12
Async XLA Ops:
  122.1 4.3 %copy-start = (f32[2]{0:T(128)S(1)}, f32[2]{0:T(128)}, u32[]{:S(2)}) copy-start(f32[2]{0:T(128)} %get-tuple-element.5) | copy-start | bytes 28

commit v8 on v7

--- a/solution.py
+++ b/solution.py
@@ -447,10 +447,10 @@
     make_delta(0)
     make_delta(1)
     down(2)
+    pass_delta(1)
+    pass_delta(0)
     relay(3)
     down(3)
-    pass_delta(0)
-    pass_delta(1)
     make_delta(2)
     add_grad(0)
     make_delta(3)

time: 127 us -> 125 us (0.984)
  Pallas kernels: 121 us -> 119 us
    pallas_call x1, Pallas kernels: 121 us -> 119 us  [shards(): pl.pallas_call(kernel, out_shape=(jax.ShapeDtypeStruct((FF, W), F32), jax...]
where the time goes in v8:
time: 125 us; the launch traced here: 124 us
  Pallas kernels  119 us (95%)
  local copies, waits for them, and re-layouts  4.76 us (4%)
    pallas_call x1, Pallas kernels, shards(): pl.pallas_call(kernel, out_shape=(jax.ShapeDtypeStruct((FF, W), F32), jax...  119 us
    unnamed x4, local copies, waits for them, and re-layouts  4.76 us

profile of v8, /device:TPU:1, one launch (start us, length us, event | category | flops | bytes accessed | tf_op | source)
XLA Modules:
  0.0 124.3 jit_solution(7540640585042245989)
XLA Ops:
  0.6 118.9 %shard_map.86 = (f32[1792,512]{1,0:T(8,128)}, f32[2]{0:T(128)}) custom-call(s32[2,8]{1,0:T(2,128)} %lens.1, f32[64,128]{1,0:T(8,128)} %bitcast.1, bf16[256,512]{1,0:T(8,128)(2,1)} %tok_in.1, bf16[512,1792]{1,0:T(8,128)(2,1)} %gw.1, bf16[512,1792]{1,0:T(8,128)(2,1)} %uw.1, bf16[1792,512]{1,0:T(8,128)(2,1)} %wf_in.1, bf16[1792,512]{1,0:T(8,128)(2,1)} %wl_in.1), custom_call_target="tpu_custom_call" | custom-call | tf_op jit(solution)/shard_map/pallas_call | solution.py:486
  119.5 0.0 copy-start
  119.5 4.2 %copy.11 = f32[1792,512]{1,0:T(8,128)} copy(f32[1792,512]{1,0:T(8,128)} %get-tuple-element.4) | data formatting | bytes 7340032
  123.8 0.0 copy-done
  123.8 0.5 copy.12
Async XLA Ops:
  119.5 4.3 %copy-start = (f32[2]{0:T(128)S(1)}, f32[2]{0:T(128)}, u32[]{:S(2)}) copy-start(f32[2]{0:T(128)} %get-tuple-element.5) | copy-start | bytes 28
